TPU v7x, 128 devices: a whole 4x4x4 slice. The times are simulated.
128 devices in a mesh: row: 16 (over z_lo, y, core), col: 8 (over z_hi, x).
Axes of the slice: x: 4, y: 4, z: 4 (z_hi: 2, z_lo: 2; z = z_hi * 2 + z_lo), core: 2. Of those that a mesh axis runs over, the one named last changes fastest.
Arguments:
- a_values: float32 [8192, 8192], P('row', 'col'), may hold values from -6 to 6
- a_mask: int32 [64, 64], P('row', 'col'), may hold values from 0 to 1, as said below
- b_values: float32 [8192, 8192], P('row', 'col'), may hold values from -0.5 to 0.5
- b_mask: int32 [64, 64], P('row', 'col'), may hold values from 0 to 1, as said below
- keep: int32 [64, 64, 64], P('row', None, 'col'), may hold values from 0 to 1, as said below
Outputs:
- product: float32 [8192, 8192], P('row', 'col')
Inputs may be any that keep to these rules, and one draw needn't show every extreme that they name: `keep`: 0 means the triple is filtered out, 1 that it counts. `a_mask`: 1 means the block is stored; on one device at most 20 blocks are stored, and some device holds exactly 20. `b_mask`: 1 means the block is stored; on one device at most 20 blocks are stored, and some device holds exactly 20.
All inputs are finite; a program needn't handle non-finite values.
Results may differ from a plain program's by a relative error of at most 0.000071.
Values sent between devices are 32-bit elements; how exact they have to be, the bound alone decides.
No kernel may reach another device: no remote copies, remote signals or barrier semaphores. Data moves between devices by JAX's collectives and lax.ppermute only.
A program may use at most 384 MiB of HBM per device.

v0:
```python
import jax
import jax.numpy as jnp
from jax import lax
from jax.sharding import PartitionSpec as P


def per_device(a_values, a_mask, b_values, b_mask, keep):
    row_blocks, inner_local = a_mask.shape
    inner_rows, col_blocks = b_mask.shape
    width = a_values.shape[0] // row_blocks
    first = (
        a_values.reshape(row_blocks, width, inner_local, width)
        * a_mask.astype(jnp.float32)[:, None, :, None]
    ).reshape(a_values.shape)
    first_whole = lax.all_gather(first, "col", axis=1, tiled=True)
    second = (
        b_values.reshape(inner_rows, width, col_blocks, width)
        * b_mask.astype(jnp.float32)[:, None, :, None]
    ).reshape(b_values.shape)
    weights = jnp.repeat(keep.astype(jnp.float32), width, axis=1)
    piece = lax.all_gather(second, "row", axis=0, tiled=True)
    count = piece.shape[0]
    shaped = first_whole.reshape(row_blocks, width, count)
    results = []
    for column in range(col_blocks):
        masked = (shaped * weights[:, None, :, column]).reshape(row_blocks * width, count)
        results.append(
            jnp.dot(
                masked,
                piece[:, column * width : (column + 1) * width],
                precision=lax.Precision.HIGHEST,
                preferred_element_type=jnp.float32,
            )
        )
    return jnp.concatenate(results, axis=1)


def solution(mesh):
    return jax.shard_map(
        per_device,
        mesh=mesh,
        in_specs=(
            P("row", "col"),
            P("row", "col"),
            P("row", "col"),
            P("row", "col"),
            P("row", None, "col"),
        ),
        out_specs=P("row", "col"),
        check_vma=False,
    )
```

profile of v0, /device:TPU:1, one launch (start us, length us, event | category | flops | bytes accessed | tf_op | source)
XLA Modules:
  0.0 541.8 jit_solution(7089609412667732679)
XLA Ops:
  6.5 0.0 copy-start.1
  6.5 0.0 all-gather.3.cloned.1.call-start
  6.5 0.7 convert_element_type.9
  7.2 0.2 mul.126
  7.4 3.6 bitcast_multiply_fusion.9
  11.1 0.0 all-gather.3.cloned.1.call-update
  11.1 0.0 all-gather.5.cloned.1.call-start
  11.1 0.7 convert_element_type.11
  11.8 0.2 mul.133
  12.0 3.6 bitcast_multiply_fusion.8
  15.6 0.0 all-gather.5.cloned.1.call-update
  15.7 0.0 copy-done.1
  15.7 0.3 broadcast_in_dim.2
  16.0 0.4 reshape.36
  16.5 0.1 slice_bitcast_fusion
  16.5 183.4 %all-gather.3.cloned.1.call-done = f32[512,8192]{1,0:T(8,128)} async-done(((f32[512,1024]{1,0:T(8,128)}), f32[512,8192]{1,0:T(8,128)}) %all-gather.3.cloned.1.call-update) | async-done | bytes 16777232 | tf_op jit(solution)/shard_map/all_gather | solution.py:15
  200.0 51.5 %bitcast_multiply_fusion = (f32[512,8192]{1,0:T(8,128)}, f32[512,8192]{1,0:T(8,128)}, f32[512,8192]{1,0:T(8,128)}, f32[512,8192]{1,0:T(8,128)}, f32[512,8192]{1,...) fusion(f32[512,8192]{1,0:T(8,128)} %all-gather.3.cloned.1.call-done, ...), kind=kLoop, calls=%fused_computation | loop fusion | flops 33554432 | bytes 152043520 | tf_op jit(solution)/shard_map/mul | solution.py:26
  251.4 119.5 %all-gather.5.cloned.1.call-done = f32[8192,1024]{1,0:T(8,128)} async-done(((f32[512,1024]{1,0:T(8,128)}), f32[8192,1024]{1,0:T(8,128)}) %all-gather.5.cloned.1.call-update) | async-done | bytes 33554448 | tf_op jit(solution)/shard_map/all_gather | solution.py:21
  370.9 0.0 copy-start
  370.9 18.5 %fusion.16 = f32[512,1024]{0,1:T(8,128)S(1)} fusion(f32[512,8192]{1,0:T(8,128)} %get-tuple-element.12, f32[8192,1024]{1,0:T(8,128)} %all-gather.5.cloned.1.call-done), kind=kOutput, calls=%fused_computation.26 | convolution fusion | flops 6442450944 | bytes 21233664 | tf_op jit(solution)/shard_map/dot_general | solution.py:28
  389.4 0.0 copy-done
  389.4 30.7 %fusion.19 = f32[512,1024]{0,1:T(8,128)S(1)} fusion(f32[512,1024]{0,1:T(8,128)S(1)} %fusion.16, f32[512,8192]{1,0:T(8,128)S(1)} %copy-done, f32[8192,1024]{1,0:T(8,128)} %all-gather.5.cloned.1.call-done), kind=kOutput, calls=%fused_computation.27 | convolution fusion | flops 6442450944 | bytes 21233664 | tf_op jit(solution)/shard_map/dot_general | solution.py:28
  420.1 0.0 slice-start.4
  420.1 0.0 slice-start.5
  420.1 18.2 %fusion.22 = f32[512,1024]{0,1:T(8,128)S(1)} fusion(f32[512,1024]{0,1:T(8,128)S(1)} %fusion.19, f32[512,8192]{1,0:T(8,128)} %get-tuple-element.10, f32[8192,1024]{1,0:T(8,128)} %all-gather.5.cloned.1.call-done), kind=kOutput, calls=%fused_computation.28 | convolution fusion | flops 6442450944 | bytes 21233664 | tf_op jit(solution)/shard_map/dot_general | solution.py:28
  438.3 0.0 slice-start.6
  438.3 0.0 slice-start.7
  438.3 18.6 %fusion.25 = f32[512,1024]{0,1:T(8,128)S(1)} fusion(f32[512,1024]{0,1:T(8,128)S(1)} %fusion.22, f32[512,8192]{1,0:T(8,128)} %get-tuple-element.9, f32[8192,1024]{1,0:T(8,128)} %all-gather.5.cloned.1.call-done), kind=kOutput, calls=%fused_computation.29 | convolution fusion | flops 6442450944 | bytes 21233664 | tf_op jit(solution)/shard_map/dot_general | solution.py:28
  456.9 0.0 slice-done.4
  456.9 0.0 slice-done.5
  456.9 0.0 slice-done.6
  456.9 0.0 slice-done.7
  456.9 19.7 %fusion.28 = f32[512,1024]{0,1:T(8,128)S(1)} fusion(f32[512,1024]{0,1:T(8,128)S(1)} %fusion.25, f32[512,8192]{1,0:T(8,128)S(1)} %bitcast.55, f32[8192,1024]{1,0:T(8,128)} %all-gather.5.cloned.1.call-done), kind=kOutput, calls=%fused_computation.30 | convolution fusion | flops 6442450944 | bytes 21233664 | tf_op jit(solution)/shard_map/dot_general | solution.py:28
  476.6 0.0 slice-start
  476.6 0.0 slice-start.1
  476.6 18.2 %fusion.31 = f32[512,1024]{0,1:T(8,128)S(1)} fusion(f32[512,1024]{0,1:T(8,128)S(1)} %fusion.28, f32[512,8192]{1,0:T(8,128)} %get-tuple-element.7, f32[8192,1024]{1,0:T(8,128)} %all-gather.5.cloned.1.call-done), kind=kOutput, calls=%fused_computation.31 | convolution fusion | flops 6442450944 | bytes 21233664 | tf_op jit(solution)/shard_map/dot_general | solution.py:28
  494.8 0.0 slice-start.2
  494.8 0.0 slice-start.3
  494.8 18.4 %fusion.34 = f32[512,1024]{0,1:T(8,128)S(1)} fusion(f32[512,1024]{0,1:T(8,128)S(1)} %fusion.31, f32[512,8192]{1,0:T(8,128)} %get-tuple-element.6, f32[8192,1024]{1,0:T(8,128)} %all-gather.5.cloned.1.call-done), kind=kOutput, calls=%fused_computation.32 | convolution fusion | flops 6442450944 | bytes 21233664 | tf_op jit(solution)/shard_map/dot_general | solution.py:28
  513.2 0.0 slice-done
  513.2 0.0 slice-done.1
  513.2 0.0 slice-done.2
  513.3 0.0 slice-done.3
  513.3 19.5 %fusion.37 = f32[512,1024]{0,1:T(8,128)S(1)} fusion(f32[512,1024]{0,1:T(8,128)S(1)} %fusion.34, f32[512,8192]{1,0:T(8,128)S(1)} %bitcast.53, f32[8192,1024]{1,0:T(8,128)} %all-gather.5.cloned.1.call-done), kind=kOutput, calls=%fused_computation.33 | convolution fusion | flops 6442450944 | bytes 21233664 | tf_op jit(solution)/shard_map/dot_general | solution.py:28
  532.8 1.8 copy.7
  (4 shorter events, 0.0 us)
Async XLA Ops:
  6.5 9.1 %copy-start.1 = (s32[4,64,8]{1,2,0:T(8,128)S(1)}, s32[4,64,8]{1,2,0:T(8,128)}, u32[]{:S(2)}) copy-start(s32[4,64,8]{1,2,0:T(8,128)} %param.9) | copy-start | bytes 24580
  6.5 193.4 %all-gather.3.cloned.1.call-start = ((), (), s32[]{:S(2)}) async-start(), calls=%async_computation | async-start | bytes 18874368 | tf_op jit(solution)/shard_map/all_gather | solution.py:15
  11.1 359.8 %all-gather.5.cloned.1.call-start = ((), (), s32[]{:S(2)}) async-start(), calls=%async_computation.1 | async-start | bytes 35651584 | tf_op jit(solution)/shard_map/all_gather | solution.py:21
  370.9 18.5 %copy-start = (f32[512,8192]{1,0:T(8,128)S(1)}, f32[512,8192]{1,0:T(8,128)}, u32[]{:S(2)}) copy-start(f32[512,8192]{1,0:T(8,128)} %get-tuple-element.11) | copy-start | bytes 50331652
  420.1 36.8 %slice-start.4 = ((s8[16777216]{0:T(1024)(128)(4,1)}), s8[4194304]{0:T(1024)(128)(4,1)S(1)}, s32[]{:S(2)}) async-start(s8[16777216]{0:T(1024)(128)(4,1)} %bitcast.54), calls=%async_computation.6 | async-start | bytes 8388608
  420.1 36.8 %slice-start.5 = ((s8[16777216]{0:T(1024)(128)(4,1)}), s8[4194304]{0:T(1024)(128)(4,1)S(1)}, s32[]{:S(2)}) async-start(s8[16777216]{0:T(1024)(128)(4,1)} %bitcast.54), calls=%async_computation.7 | async-start | bytes 8388608
  438.3 18.6 %slice-start.6 = ((s8[16777216]{0:T(1024)(128)(4,1)}), s8[4194304]{0:T(1024)(128)(4,1)S(1)}, s32[]{:S(2)}) async-start(s8[16777216]{0:T(1024)(128)(4,1)} %bitcast.54), calls=%async_computation.8 | async-start | bytes 8388608
  438.3 18.6 %slice-start.7 = ((s8[16777216]{0:T(1024)(128)(4,1)}), s8[4194304]{0:T(1024)(128)(4,1)S(1)}, s32[]{:S(2)}) async-start(s8[16777216]{0:T(1024)(128)(4,1)} %bitcast.54), calls=%async_computation.9 | async-start | bytes 8388608
  476.6 36.6 %slice-start = ((s8[16777216]{0:T(1024)(128)(4,1)}), s8[4194304]{0:T(1024)(128)(4,1)S(1)}, s32[]{:S(2)}) async-start(s8[16777216]{0:T(1024)(128)(4,1)} %bitcast.52), calls=%async_computation.2 | async-start | bytes 8388608
  476.6 36.6 %slice-start.1 = ((s8[16777216]{0:T(1024)(128)(4,1)}), s8[4194304]{0:T(1024)(128)(4,1)S(1)}, s32[]{:S(2)}) async-start(s8[16777216]{0:T(1024)(128)(4,1)} %bitcast.52), calls=%async_computation.3 | async-start | bytes 8388608
  494.8 18.4 %slice-start.2 = ((s8[16777216]{0:T(1024)(128)(4,1)}), s8[4194304]{0:T(1024)(128)(4,1)S(1)}, s32[]{:S(2)}) async-start(s8[16777216]{0:T(1024)(128)(4,1)} %bitcast.52), calls=%async_computation.4 | async-start | bytes 8388608
  494.8 18.4 %slice-start.3 = ((s8[16777216]{0:T(1024)(128)(4,1)}), s8[4194304]{0:T(1024)(128)(4,1)S(1)}, s32[]{:S(2)}) async-start(s8[16777216]{0:T(1024)(128)(4,1)} %bitcast.52), calls=%async_computation.5 | async-start | bytes 8388608
Sparse Core Ops, SparseCore 0:
  11.2 188.7 all-gather.2
  201.7 169.1 all-gather.4
where the time goes:
time: 550 us; the launch traced here: 542 us
  waiting for transfers between devices  303 us (55%)
  matrix products  162 us (29%)
  other arithmetic  60.1 us (11%)
  between operations  14.1 us (3%)
    all_gather x1, waiting for transfers between devices, per_device(): first_whole = lax.all_gather(first, 'col', axis=1, tiled=True)  183 us
    dot_general x8, matrix products, per_device(): jnp.dot(masked, piece[:, column * width:(column + 1) * width], precision=...  162 us
    all_gather x1, waiting for transfers between devices, per_device(): piece = lax.all_gather(second, 'row', axis=0, tiled=True)  119 us
    mul x1, other arithmetic, per_device(): shaped * weights[:, None, :, column]  51.5 us
  transfers between devices with their start and end apart: 2, of which 2 were waited for; matrix products, arithmetic and copies ran while one was open for 10% of the time, Pallas kernels for 0%

commit v1 on v0

--- a/solution.py
+++ b/solution.py
@@ -18,7 +18,10 @@
         * b_mask.astype(jnp.float32)[:, None, :, None]
     ).reshape(b_values.shape)
     weights = jnp.repeat(keep.astype(jnp.float32), width, axis=1)
-    piece = lax.all_gather(second, "row", axis=0, tiled=True)
+    n_dev = lax.axis_size("row")
+    parts = jnp.stack([second for _ in range(n_dev)])
+    parts = lax.all_to_all(parts, "row", split_axis=0, concat_axis=0)
+    piece = jnp.concatenate(parts, axis=0)
     count = piece.shape[0]
     shaped = first_whole.reshape(row_blocks, width, count)
     results = []

time: 550 us -> 765 us (1.39)
  waiting for transfers between devices: 303 us -> 506 us
  local copies, waits for them, and re-layouts: 3.08 us -> 14.4 us
    all_gather x1, waiting for transfers between devices: 183 us -> 506 us  [per_device(): first_whole = lax.all_gather(first, 'col', axis=1, tiled=True)]
    all_gather x1 -> x0, waiting for transfers between devices: 119 us -> none  [per_device(): piece = lax.all_gather(second, 'row', axis=0, tiled=True)]
    another operation x0 -> x1, local copies, waits for them, and re-layouts: none -> 11.4 us  [per_device(): parts = jnp.stack([second for _ in range(n_dev)])]
  transfers between devices with their start and end apart: 2 -> 2, of which waited for: 2 -> 1; matrix products, arithmetic and copies ran while one was open for 10% -> 7% of each run, Pallas kernels for 0% -> 0%
where the time goes in v1:
time: 765 us; the launch traced here: 756 us
  waiting for transfers between devices  506 us (66%)
  matrix products  162 us (21%)
  other arithmetic  53 us (7%)
  local copies, waits for them, and re-layouts  14.4 us (2%)
  between operations  14.1 us (2%)
    all_gather x1, waiting for transfers between devices, per_device(): first_whole = lax.all_gather(first, 'col', axis=1, tiled=True)  506 us
    dot_general x8, matrix products, per_device(): jnp.dot(masked, piece[:, column * width:(column + 1) * width], precision=...  162 us
    mul x1, other arithmetic, per_device(): shaped * weights[:, None, :, column]  47.9 us
  transfers between devices with their start and end apart: 2, of which 1 were waited for; matrix products, arithmetic and copies ran while one was open for 7% of the time, Pallas kernels for 0%

profile of v1, /device:TPU:1, one launch (start us, length us, event | category | flops | bytes accessed | tf_op | source)
XLA Modules:
  0.0 756.5 jit_solution(15369945244902268368)
XLA Ops:
  6.5 0.7 convert_element_type.11
  7.2 0.2 mul.134
  7.4 2.3 bitcast_multiply_fusion.8
  9.7 11.4 %stack.3 = f32[16,512,1024]{2,1,0:T(8,128)} broadcast(f32[512,1024]{1,0:T(8,128)S(1)} %bitcast_multiply_fusion.8), dimensions={1,2} | broadcast | bytes 35651584 | tf_op jit(solution)/shard_map/stack | solution.py:22
  21.1 0.0 copy-start.3
  21.1 0.0 copy-start.1
  21.1 0.0 copy-start.2
  21.1 7.5 all-to-all-start
  28.6 0.0 all-gather.2.cloned.1.call-start
  28.6 0.0 copy-done.3
  28.6 0.2 mul.127
  28.9 0.0 copy-done.1
  28.9 2.0 bitcast_multiply_fusion.9
  30.9 0.0 all-gather.2.cloned.1.call-update
  30.9 0.0 copy-done.2
  31.0 0.3 broadcast_in_dim.2
  31.3 0.4 reshape.41
  31.7 0.1 slice_bitcast_fusion
  31.8 505.8 %all-gather.2.cloned.1.call-done = f32[512,8192]{1,0:T(8,128)} async-done(((f32[512,1024]{1,0:T(8,128)}), f32[512,8192]{1,0:T(8,128)}) %all-gather.2.cloned.1.call-update) | async-done | bytes 16777232 | tf_op jit(solution)/shard_map/all_gather | solution.py:15
  537.6 47.9 %bitcast_multiply_fusion = (f32[512,8192]{1,0:T(8,128)}, f32[512,8192]{1,0:T(8,128)}, f32[512,8192]{1,0:T(8,128)}, f32[512,8192]{1,0:T(8,128)}, f32[512,8192]{1,...) fusion(f32[512,8192]{1,0:T(8,128)} %all-gather.2.cloned.1.call-done, ...), kind=kLoop, calls=%fused_computation | loop fusion | flops 33554432 | bytes 152043520 | tf_op jit(solution)/shard_map/mul | solution.py:29
  585.5 0.0 all-to-all-done
  585.5 0.0 copy-start
  585.5 18.5 %fusion.16 = f32[512,1024]{0,1:T(8,128)S(1)} fusion(f32[512,8192]{1,0:T(8,128)} %get-tuple-element.12, f32[8192,1024]{1,0:T(8,128)} %bitcast.2), kind=kOutput, calls=%fused_computation.26 | convolution fusion | flops 6442450944 | bytes 21233664 | tf_op jit(solution)/shard_map/dot_general | solution.py:31
  604.0 0.0 copy-done
  604.0 30.7 %fusion.19 = f32[512,1024]{0,1:T(8,128)S(1)} fusion(f32[512,1024]{0,1:T(8,128)S(1)} %fusion.16, f32[512,8192]{1,0:T(8,128)S(1)} %copy-done, f32[8192,1024]{1,0:T(8,128)} %bitcast.2), kind=kOutput, calls=%fused_computation.27 | convolution fusion | flops 6442450944 | bytes 21233664 | tf_op jit(solution)/shard_map/dot_general | solution.py:31
  634.7 0.0 slice-start.4
  634.7 0.0 slice-start.5
  634.7 18.2 %fusion.22 = f32[512,1024]{0,1:T(8,128)S(1)} fusion(f32[512,1024]{0,1:T(8,128)S(1)} %fusion.19, f32[512,8192]{1,0:T(8,128)} %get-tuple-element.10, f32[8192,1024]{1,0:T(8,128)} %bitcast.2), kind=kOutput, calls=%fused_computation.28 | convolution fusion | flops 6442450944 | bytes 21233664 | tf_op jit(solution)/shard_map/dot_general | solution.py:31
  652.9 0.0 slice-start.6
  652.9 0.0 slice-start.7
  652.9 18.6 %fusion.25 = f32[512,1024]{0,1:T(8,128)S(1)} fusion(f32[512,1024]{0,1:T(8,128)S(1)} %fusion.22, f32[512,8192]{1,0:T(8,128)} %get-tuple-element.9, f32[8192,1024]{1,0:T(8,128)} %bitcast.2), kind=kOutput, calls=%fused_computation.29 | convolution fusion | flops 6442450944 | bytes 21233664 | tf_op jit(solution)/shard_map/dot_general | solution.py:31
  671.5 0.0 slice-done.4
  671.5 0.0 slice-done.5
  671.5 0.0 slice-done.6
  671.5 0.0 slice-done.7
  671.6 19.7 %fusion.28 = f32[512,1024]{0,1:T(8,128)S(1)} fusion(f32[512,1024]{0,1:T(8,128)S(1)} %fusion.25, f32[512,8192]{1,0:T(8,128)S(1)} %bitcast.56, f32[8192,1024]{1,0:T(8,128)} %bitcast.2), kind=kOutput, calls=%fused_computation.30 | convolution fusion | flops 6442450944 | bytes 21233664 | tf_op jit(solution)/shard_map/dot_general | solution.py:31
  691.2 0.0 slice-start
  691.2 0.0 slice-start.1
  691.3 18.2 %fusion.31 = f32[512,1024]{0,1:T(8,128)S(1)} fusion(f32[512,1024]{0,1:T(8,128)S(1)} %fusion.28, f32[512,8192]{1,0:T(8,128)} %get-tuple-element.7, f32[8192,1024]{1,0:T(8,128)} %bitcast.2), kind=kOutput, calls=%fused_computation.31 | convolution fusion | flops 6442450944 | bytes 21233664 | tf_op jit(solution)/shard_map/dot_general | solution.py:31
  709.4 0.0 slice-start.2
  709.5 0.0 slice-start.3
  709.5 18.4 %fusion.34 = f32[512,1024]{0,1:T(8,128)S(1)} fusion(f32[512,1024]{0,1:T(8,128)S(1)} %fusion.31, f32[512,8192]{1,0:T(8,128)} %get-tuple-element.6, f32[8192,1024]{1,0:T(8,128)} %bitcast.2), kind=kOutput, calls=%fused_computation.32 | convolution fusion | flops 6442450944 | bytes 21233664 | tf_op jit(solution)/shard_map/dot_general | solution.py:31
  727.9 0.0 slice-done
  727.9 0.0 slice-done.1
  727.9 0.0 slice-done.2
  727.9 0.0 slice-done.3
  727.9 19.5 %fusion.37 = f32[512,1024]{0,1:T(8,128)S(1)} fusion(f32[512,1024]{0,1:T(8,128)S(1)} %fusion.34, f32[512,8192]{1,0:T(8,128)S(1)} %bitcast.54, f32[8192,1024]{1,0:T(8,128)} %bitcast.2), kind=kOutput, calls=%fused_computation.33 | convolution fusion | flops 6442450944 | bytes 21233664 | tf_op jit(solution)/shard_map/dot_general | solution.py:31
  747.4 1.8 copy.7
  (5 shorter events, 0.0 us)
Async XLA Ops:
  21.1 7.5 copy-start.3
  21.1 7.8 %copy-start.1 = (f32[512,1024]{1,0:T(8,128)S(1)}, f32[512,1024]{1,0:T(8,128)}, u32[]{:S(2)}) copy-start(f32[512,1024]{1,0:T(8,128)} %param.5) | copy-start | bytes 6291460
  21.1 9.8 %copy-start.2 = (s32[4,64,8]{1,2,0:T(8,128)S(1)}, s32[4,64,8]{1,2,0:T(8,128)}, u32[]{:S(2)}) copy-start(s32[4,64,8]{1,2,0:T(8,128)} %param.9) | copy-start | bytes 24580
  21.1 564.4 %all-to-all-start = ((f32[16,512,1024]{2,1,0:T(8,128)}), f32[16,512,1024]{2,1,0:T(8,128)}, u32[]{:S(2)}, u32[]{:S(2)}) async-start(f32[16,512,1024]{2,1,0:T(8,128)} %stack.3), calls=%async_computation | async-start | bytes 67108864 | tf_op jit(solution)/shard_map/all_to_all | solution.py:23
  28.6 509.0 %all-gather.2.cloned.1.call-start = ((), (), s32[]{:S(2)}) async-start(), calls=%async_computation.1 | async-start | bytes 18874368 | tf_op jit(solution)/shard_map/all_gather | solution.py:15
  585.5 18.5 %copy-start = (f32[512,8192]{1,0:T(8,128)S(1)}, f32[512,8192]{1,0:T(8,128)}, u32[]{:S(2)}) copy-start(f32[512,8192]{1,0:T(8,128)} %get-tuple-element.11) | copy-start | bytes 50331652
  634.7 36.8 %slice-start.4 = ((s8[16777216]{0:T(1024)(128)(4,1)}), s8[4194304]{0:T(1024)(128)(4,1)S(1)}, s32[]{:S(2)}) async-start(s8[16777216]{0:T(1024)(128)(4,1)} %bitcast.55), calls=%async_computation.6 | async-start | bytes 8388608
  634.7 36.8 %slice-start.5 = ((s8[16777216]{0:T(1024)(128)(4,1)}), s8[4194304]{0:T(1024)(128)(4,1)S(1)}, s32[]{:S(2)}) async-start(s8[16777216]{0:T(1024)(128)(4,1)} %bitcast.55), calls=%async_computation.7 | async-start | bytes 8388608
  652.9 18.6 %slice-start.6 = ((s8[16777216]{0:T(1024)(128)(4,1)}), s8[4194304]{0:T(1024)(128)(4,1)S(1)}, s32[]{:S(2)}) async-start(s8[16777216]{0:T(1024)(128)(4,1)} %bitcast.55), calls=%async_computation.8 | async-start | bytes 8388608
  652.9 18.6 %slice-start.7 = ((s8[16777216]{0:T(1024)(128)(4,1)}), s8[4194304]{0:T(1024)(128)(4,1)S(1)}, s32[]{:S(2)}) async-start(s8[16777216]{0:T(1024)(128)(4,1)} %bitcast.55), calls=%async_computation.9 | async-start | bytes 8388608
  691.2 36.6 %slice-start = ((s8[16777216]{0:T(1024)(128)(4,1)}), s8[4194304]{0:T(1024)(128)(4,1)S(1)}, s32[]{:S(2)}) async-start(s8[16777216]{0:T(1024)(128)(4,1)} %bitcast.53), calls=%async_computation.2 | async-start | bytes 8388608
  691.2 36.6 %slice-start.1 = ((s8[16777216]{0:T(1024)(128)(4,1)}), s8[4194304]{0:T(1024)(128)(4,1)S(1)}, s32[]{:S(2)}) async-start(s8[16777216]{0:T(1024)(128)(4,1)} %bitcast.53), calls=%async_computation.3 | async-start | bytes 8388608
  709.4 18.4 %slice-start.2 = ((s8[16777216]{0:T(1024)(128)(4,1)}), s8[4194304]{0:T(1024)(128)(4,1)S(1)}, s32[]{:S(2)}) async-start(s8[16777216]{0:T(1024)(128)(4,1)} %bitcast.53), calls=%async_computation.4 | async-start | bytes 8388608
  709.5 18.4 %slice-start.3 = ((s8[16777216]{0:T(1024)(128)(4,1)}), s8[4194304]{0:T(1024)(128)(4,1)S(1)}, s32[]{:S(2)}) async-start(s8[16777216]{0:T(1024)(128)(4,1)} %bitcast.53), calls=%async_computation.5 | async-start | bytes 8388608
Sparse Core Ops, SparseCore 0:
  31.8 505.7 all-gather.1
